TPU v7x, 32 devices: a whole 2x2x4 slice. The times are simulated.
32 devices in a mesh: prow: 8 (over z, y), pcol: 4 (over x, core).
Axes of the slice: x: 2, y: 2, z: 4, core: 2. Of those that a mesh axis runs over, the one named last changes fastest.
Arguments:
- paper_x: bfloat16 [8192, 768], P(('prow', 'pcol')), may hold values from -6 to 6
- author_x: bfloat16 [4096, 768], P(('pcol', 'prow')), may hold values from -6 to 6
- w_self: bfloat16 [768, 768], replicated, may hold values from -0.21875 to 0.21875
- w_rel: bfloat16 [2, 768, 768], replicated, may hold values from -0.009765625 to 0.009765625
- w_two: bfloat16 [768, 768], replicated, may hold values from -0.0068359375 to 0.0068359375
- block_rows: int32 [8, 4, 32], P('prow', 'pcol'), may hold values from 0 to 7, as said below
- block_cols: int32 [8, 4, 32], P('prow', 'pcol'), may hold values from 0 to 7, as said below
- block_type: int32 [8, 4, 32], P('prow', 'pcol'), may hold values from 0 to 1
- block_count: int32 [8, 4], P('prow', 'pcol'), may hold values from 8 to 32, as said below
- block_vals: bfloat16 [8, 4, 32, 128, 128], P('prow', 'pcol'), may hold values from 0 to 1, as said below
Outputs:
- paper_hidden: bfloat16 [8192, 768], P(('prow', 'pcol'))
- author_out: bfloat16 [4096, 768], P(('pcol', 'prow'))
Inputs may be any that keep to these rules, and one draw needn't show every extreme that they name: `block_rows`: within one tile the live and dead slots name distinct positions; block rows are below 8. `block_cols`: block columns are below 8; with block_rows, positions of one tile are distinct. `block_count`: slots 0 to count - 1 of a tile are live; some tile holds 32 live slots and some tile 32 // 4 in every draw. `block_vals`: every entry is 0 or 1.
All inputs are finite; a program needn't handle non-finite values.
Results may differ from a plain program's by a relative error of at most 0.0041.
Values may be sent and summed in bfloat16 or wider, within the bound.
A program may use at most 64 MiB of HBM per device.

v0:
```python
import jax
import jax.numpy as jnp
from jax import lax
from jax.sharding import PartitionSpec as P

GROUP = 16


def per_device(
    paper_x,
    author_x,
    w_self,
    w_rel,
    w_two,
    block_rows,
    block_cols,
    block_type,
    block_count,
    block_vals,
):
    slots = block_rows.shape[2]
    side = block_vals.shape[3]
    width = paper_x.shape[1]
    relations = w_rel.shape[0]
    groups = slots // GROUP
    own_rows = paper_x.shape[0]
    row_ids = block_rows.reshape(groups, GROUP)
    col_ids = block_cols.reshape(groups, GROUP)
    type_ids = block_type.reshape(groups, GROUP)
    live = (
        (jnp.arange(slots, dtype=jnp.int32) < block_count.reshape(()))
        .astype(jnp.float32)
        .reshape(groups, GROUP)
    )
    contents = block_vals.reshape(groups, GROUP, side, side)
    self_term = jnp.dot(paper_x, w_self, preferred_element_type=jnp.float32)
    authors = lax.all_gather(author_x, "prow", axis=0, tiled=True)
    messages = jnp.stack(
        [
            jnp.dot(authors, w_rel[index], preferred_element_type=jnp.float32)
            for index in range(relations)
        ]
    ).astype(jnp.bfloat16)
    col_blocks = messages.shape[1] // side
    row_blocks = own_rows * lax.axis_size("pcol") // side
    table = messages.reshape(relations * col_blocks, side, width)
    row_range = jnp.arange(row_blocks, dtype=jnp.int32)
    col_range = jnp.arange(col_blocks, dtype=jnp.int32)

    def first_hop(total, item):
        rows_now, cols_now, types_now, mask_now, content_now = item
        picked = table[types_now * col_blocks + cols_now]
        product = jnp.einsum(
            "kpa,kaf->kpf", content_now, picked, preferred_element_type=jnp.float32
        )
        placing = (rows_now[:, None] == row_range[None, :]).astype(jnp.float32) * mask_now[:, None]
        return (
            total + jnp.einsum("kr,kpf->rpf", placing, product, precision=lax.Precision.HIGHEST),
            None,
        )

    start = jnp.zeros((row_blocks, side, width), jnp.float32)
    partial_value, _ = lax.scan(first_hop, start, (row_ids, col_ids, type_ids, live, contents))
    partial_value = partial_value.reshape(row_blocks * side, width)
    summed = lax.psum_scatter(partial_value, "pcol", scatter_dimension=0, tiled=True)
    paper_hidden = jnp.maximum(self_term + summed, 0.0).astype(jnp.bfloat16)
    outgoing = jnp.dot(paper_hidden, w_two, preferred_element_type=jnp.float32).astype(jnp.bfloat16)
    paper_rows = lax.all_gather(outgoing, "pcol", axis=0, tiled=True).reshape(
        row_blocks, side, width
    )

    def second_hop(total, item):
        rows_now, cols_now, mask_now, content_now = item
        picked = paper_rows[rows_now]
        product = jnp.einsum(
            "kpa,kpf->kaf", content_now, picked, preferred_element_type=jnp.float32
        )
        placing = (cols_now[:, None] == col_range[None, :]).astype(jnp.float32) * mask_now[:, None]
        return (
            total + jnp.einsum("kc,kaf->caf", placing, product, precision=lax.Precision.HIGHEST),
            None,
        )

    start_two = jnp.zeros((col_blocks, side, width), jnp.float32)
    author_part, _ = lax.scan(second_hop, start_two, (row_ids, col_ids, live, contents))
    author_total = lax.psum_scatter(
        author_part.reshape(col_blocks * side, width), "prow", scatter_dimension=0, tiled=True
    )
    return (paper_hidden, author_total.astype(jnp.bfloat16))


def solution(mesh):
    return jax.shard_map(
        per_device,
        mesh=mesh,
        in_specs=(
            P(("prow", "pcol"), None),
            P(("pcol", "prow"), None),
            P(),
            P(),
            P(),
            P("prow", "pcol", None),
            P("prow", "pcol", None),
            P("prow", "pcol", None),
            P("prow", "pcol"),
            P("prow", "pcol", None, None, None),
        ),
        out_specs=(P(("prow", "pcol"), None), P(("pcol", "prow"), None)),
        check_vma=False,
    )
```

profile of v0, /device:TPU:0, one launch (start us, length us, event | category | flops | bytes accessed | tf_op | source)
XLA Modules:
  0.0 299.5 jit_solution(3397042512454895330)
XLA Ops:
  7.2 0.0 copy-start
  7.2 0.0 all-gather.3.cloned.1.call-start
  7.2 0.7 all-gather.3.cloned.1.call-update
  7.9 0.0 reduce-scatter.3.cloned.1.call-start
  8.0 0.5 broadcast.116
  8.5 1.3 reduce.9
  9.8 0.1 reshape.103
  9.9 1.3 reduce.11
  11.2 0.1 reshape.107
  11.3 1.3 reduce.10
  12.6 0.1 reshape.106
  13.4 43.8 %all-gather.3.cloned.1.call-done = bf16[1024,768]{1,0:T(8,128)(2,1)} async-done(((bf16[128,768]{1,0:T(8,128)(2,1)}), bf16[1024,768]{1,0:T(8,128)(2,1)}) %all-gather.3.cloned.1.call-update) | async-done | bytes 1572880 | tf_op jit(solution)/shard_map/all_gather | solution.py:37
  57.1 3.3 %fusion.41 = bf16[1,1024,768]{2,1,0:T(8,128)(2,1)S(1)} fusion(bf16[1024,768]{1,0:T(8,128)(2,1)} %all-gather.3.cloned.1.call-done, bf16[2,768,768]{2,1,0:T(8,128)(2,1)} %param.17), kind=kOutput, calls=%fused_computation.55 | convolution fusion | flops 1208745984 | bytes 4325376 | tf_op jit(solution)/shard_map/dot_general | solution.py:40
  60.4 0.0 copy-done.4
  60.4 0.0 copy-done.5
  60.4 1.4 fusion.42
  61.8 0.0 copy-start.1
  61.8 2.0 pad_maximum_fusion
  63.8 0.0 copy-done.1
  63.8 41.9 %while.22 = (s32[]{:T(128)}, f32[8,128,768]{2,0,1:T(8,128)}, s32[2,16]{1,0:T(2,128)S(1)}, f32[2,16]{1,0:T(2,128)S(1)}, bf16[2,16,128,128]{3,2,1,0:T(8,128)(2,1)S...) while((s32[]{:T(128)}, f32[8,128,768]{2,0,1:T(8,128)}, ...), condition=%wide.region_1.2_spmd.clone, body=%wide.region_0.1_spmd.clone.sunk | while | flops 555222400 | bytes 28840768 | solution.py:63
  63.8 4.3 %gather_fusion = bf16[16,128,768]{2,1,0:T(8,128)(2,1)} fusion(bf16[16,128,768]{2,1,0:T(8,128)(2,1)} %get-tuple-element.297, s32[1024]{0:T(1024)S(1)} %pad_clamp_fusion.4), kind=kCustom, calls=%fused_computation.clone.clone.1 | custom fusion | bytes 6291520 | tf_op jit(solution)/shard_map/while/body/eval_jaxpr/gather | solution.py:52
  68.1 5.5 %fusion.78 = f32[16,128,768]{2,1,0:T(8,128)} fusion(bf16[16,128,768]{2,1,0:T(8,128)(2,1)} %gather_fusion, bf16[2,16,128,128]{3,2,1,0:T(8,128)(2,1)S(1)} %get-tuple-element.294, s32[]{:T(128)} %get-tuple-element.280), kind=kOutput, calls=%fused_computation.7.clone.1 | convolution fusion | flops 402653184 | bytes 9961476 | tf_op jit(solution)/shard_map/while/body/eval_jaxpr/kpa,kaf->kpf/dot_general | solution.py:53
  73.6 10.9 %select_add_fusion.4 = f32[8,128,768]{2,0,1:T(8,128)} fusion(f32[8,128,768]{2,0,1:T(8,128)} %get-tuple-element.281, f32[16,128,768]{2,1,0:T(8,128)} %fusion.78, pred[]{:T(512)S(6)} %compare.6, f32[16]{0:T(128)S(1)} %fusion.79, s32[16]{0:T(128)S(1)} %fusion.80), kind=kOutput, calls=%fused_computation.6.clone.1 | convolution fusion | flops 152568064 | bytes 12583041 | tf_op jit(solution)/shard_map/while/body/eval_jaxpr/kr,kpf->rpf/dot_general | solution.py:58
  84.5 4.3 %gather_fusion = bf16[16,128,768]{2,1,0:T(8,128)(2,1)} fusion(bf16[16,128,768]{2,1,0:T(8,128)(2,1)} %get-tuple-element.297, s32[1024]{0:T(1024)S(1)} %pad_clamp_fusion.4), kind=kCustom, calls=%fused_computation.clone.clone.1 | custom fusion | bytes 6291520 | tf_op jit(solution)/shard_map/while/body/eval_jaxpr/gather | solution.py:52
  88.8 5.5 %fusion.78 = f32[16,128,768]{2,1,0:T(8,128)} fusion(bf16[16,128,768]{2,1,0:T(8,128)(2,1)} %gather_fusion, bf16[2,16,128,128]{3,2,1,0:T(8,128)(2,1)S(1)} %get-tuple-element.294, s32[]{:T(128)} %get-tuple-element.280), kind=kOutput, calls=%fused_computation.7.clone.1 | convolution fusion | flops 402653184 | bytes 9961476 | tf_op jit(solution)/shard_map/while/body/eval_jaxpr/kpa,kaf->kpf/dot_general | solution.py:53
  94.3 11.4 %select_add_fusion.4 = f32[8,128,768]{2,0,1:T(8,128)} fusion(f32[8,128,768]{2,0,1:T(8,128)} %get-tuple-element.281, f32[16,128,768]{2,1,0:T(8,128)} %fusion.78, pred[]{:T(512)S(6)} %compare.6, f32[16]{0:T(128)S(1)} %fusion.79, s32[16]{0:T(128)S(1)} %fusion.80), kind=kOutput, calls=%fused_computation.6.clone.1 | convolution fusion | flops 152568064 | bytes 12583041 | tf_op jit(solution)/shard_map/while/body/eval_jaxpr/kr,kpf->rpf/dot_general | solution.py:58
  105.7 4.6 %copy.12 = f32[8,128,768]{2,1,0:T(8,128)} copy(f32[8,128,768]{2,0,1:T(8,128)} %get-tuple-element.91) | data formatting | bytes 6291456 | tf_op jit(solution)/shard_map/while | solution.py:63
  110.3 0.0 reduce-scatter.3.cloned.1.call-update
  110.3 0.0 all-gather.5.cloned.1.call-start
  110.3 36.3 %reduce-scatter.3.cloned.1.call-done = f32[256,768]{1,0:T(8,128)} async-done(((f32[1024,768]{1,0:T(8,128)}), f32[256,768]{1,0:T(8,128)}) %reduce-scatter.3.cloned.1.call-update) | async-done | bytes 786448 | tf_op jit(solution)/shard_map/reduce_scatter | solution.py:65
  146.7 1.6 fusion.44
  148.3 0.0 copy-start.2
  148.3 2.6 convolution_convert_fusion.2
  151.0 0.0 all-gather.5.cloned.1.call-update
  151.0 0.2 reduce-scatter.5.cloned.1.call-start
  151.2 19.5 %all-gather.5.cloned.1.call-done = bf16[1024,768]{1,0:T(8,128)(2,1)} async-done(((bf16[256,768]{1,0:T(8,128)(2,1)}), bf16[1024,768]{1,0:T(8,128)(2,1)}) %all-gather.5.cloned.1.call-update) | async-done | bytes 1572880 | tf_op jit(solution)/shard_map/all_gather | solution.py:68
  170.8 0.0 copy-done.2
  170.8 41.2 %while.23 = (s32[]{:T(128)}, f32[8,128,768]{2,0,1:T(8,128)}, s32[2,16]{1,0:T(2,128)S(1)}, f32[2,16]{1,0:T(2,128)S(1)}, bf16[2,16,128,128]{3,2,1,0:T(8,128)(2,1)S...) while((s32[]{:T(128)}, f32[8,128,768]{2,0,1:T(8,128)}, ...), condition=%wide.region_4.5_spmd.clone, body=%wide.region_3.4_spmd.clone.sunk | while | flops 555222336 | bytes 28840696 | solution.py:85
  170.8 3.8 %gather_fusion.1 = bf16[16,128,768]{2,1,0:T(8,128)(2,1)} fusion(bf16[8,128,768]{2,1,0:T(8,128)(2,1)} %get-tuple-element.324, s32[1024]{0:T(1024)S(1)} %pad_clamp_fusion.5), kind=kCustom, calls=%fused_computation.1.clone.clone.1 | custom fusion | bytes 6291520 | tf_op jit(solution)/shard_map/while/body/eval_jaxpr/gather | solution.py:74
  174.6 5.6 %fusion.86 = f32[16,128,768]{2,1,0:T(8,128)} fusion(bf16[16,128,768]{2,1,0:T(8,128)(2,1)} %gather_fusion.1, bf16[2,16,128,128]{3,2,1,0:T(8,128)(2,1)S(1)} %get-tuple-element.322, s32[]{:T(128)} %get-tuple-element.309), kind=kOutput, calls=%fused_computation.32.clone.1 | convolution fusion | flops 402653184 | bytes 9961476 | tf_op jit(solution)/shard_map/while/body/eval_jaxpr/kpa,kpf->kaf/dot_general | solution.py:75
  180.2 11.0 %select_add_fusion.5 = f32[8,128,768]{2,0,1:T(8,128)} fusion(f32[8,128,768]{2,0,1:T(8,128)} %get-tuple-element.310, f32[16,128,768]{2,1,0:T(8,128)} %fusion.86, pred[]{:T(512)S(6)} %compare.7, f32[16]{0:T(128)S(1)} %fusion.87, s32[16]{0:T(128)S(1)} %fusion.88), kind=kOutput, calls=%fused_computation.31.clone.1 | convolution fusion | flops 152568064 | bytes 12583041 | tf_op jit(solution)/shard_map/while/body/eval_jaxpr/kc,kaf->caf/dot_general | solution.py:80
  191.2 3.8 %gather_fusion.1 = bf16[16,128,768]{2,1,0:T(8,128)(2,1)} fusion(bf16[8,128,768]{2,1,0:T(8,128)(2,1)} %get-tuple-element.324, s32[1024]{0:T(1024)S(1)} %pad_clamp_fusion.5), kind=kCustom, calls=%fused_computation.1.clone.clone.1 | custom fusion | bytes 6291520 | tf_op jit(solution)/shard_map/while/body/eval_jaxpr/gather | solution.py:74
  195.0 5.6 %fusion.86 = f32[16,128,768]{2,1,0:T(8,128)} fusion(bf16[16,128,768]{2,1,0:T(8,128)(2,1)} %gather_fusion.1, bf16[2,16,128,128]{3,2,1,0:T(8,128)(2,1)S(1)} %get-tuple-element.322, s32[]{:T(128)} %get-tuple-element.309), kind=kOutput, calls=%fused_computation.32.clone.1 | convolution fusion | flops 402653184 | bytes 9961476 | tf_op jit(solution)/shard_map/while/body/eval_jaxpr/kpa,kpf->kaf/dot_general | solution.py:75
  200.5 11.4 %select_add_fusion.5 = f32[8,128,768]{2,0,1:T(8,128)} fusion(f32[8,128,768]{2,0,1:T(8,128)} %get-tuple-element.310, f32[16,128,768]{2,1,0:T(8,128)} %fusion.86, pred[]{:T(512)S(6)} %compare.7, f32[16]{0:T(128)S(1)} %fusion.87, s32[16]{0:T(128)S(1)} %fusion.88), kind=kOutput, calls=%fused_computation.31.clone.1 | convolution fusion | flops 152568064 | bytes 12583041 | tf_op jit(solution)/shard_map/while/body/eval_jaxpr/kc,kaf->caf/dot_general | solution.py:80
  212.0 4.6 %copy.13 = f32[8,128,768]{2,1,0:T(8,128)} copy(f32[8,128,768]{2,0,1:T(8,128)} %get-tuple-element.92) | data formatting | bytes 6291456 | tf_op jit(solution)/shard_map/while | solution.py:85
  216.5 0.0 reduce-scatter.5.cloned.1.call-update
  216.5 74.7 %reduce-scatter.5.cloned.1.call-done = f32[128,768]{1,0:T(8,128)} async-done(((f32[1024,768]{1,0:T(8,128)}), f32[128,768]{1,0:T(8,128)}) %reduce-scatter.5.cloned.1.call-update) | async-done | bytes 393232 | tf_op jit(solution)/shard_map/reduce_scatter | solution.py:86
  291.2 1.7 convert_element_type.24
  (24 shorter events, 0.1 us)
Async XLA Ops:
  7.2 139.5 %copy-start = (bf16[768,768]{1,0:T(8,128)(2,1)S(1)}, bf16[768,768]{1,0:T(8,128)(2,1)}, u32[]{:S(2)}) copy-start(bf16[768,768]{1,0:T(8,128)(2,1)} %param.16) | copy-start | bytes 3538948
  7.2 49.9 %all-gather.3.cloned.1.call-start = ((), (), s32[]{:S(2)}) async-start(), calls=%async_computation.2 | async-start | bytes 1769472 | tf_op jit(solution)/shard_map/all_gather | solution.py:37
  7.9 138.8 %reduce-scatter.3.cloned.1.call-start = ((), (), s32[]{:S(2)}) async-start(), calls=%async_computation.3 | async-start | bytes 3932160 | tf_op jit(solution)/shard_map/reduce_scatter | solution.py:65
  57.1 3.3 %copy-start.4 = (bf16[2,768,768]{2,1,0:T(8,128)(2,1)S(1)}, bf16[2,768,768]{2,1,0:T(8,128)(2,1)}, u32[]{:S(2)}) copy-start(bf16[2,768,768]{2,1,0:T(8,128)(2,1)} %param.17) | copy-start | bytes 7077892
  57.1 3.3 %copy-start.5 = (bf16[1024,768]{1,0:T(8,128)(2,1)S(1)}, bf16[1024,768]{1,0:T(8,128)(2,1)}, u32[]{:S(2)}) copy-start(bf16[1024,768]{1,0:T(8,128)(2,1)} %all-gather.3.cloned.1.call-done) | copy-start | bytes 4718596
  61.8 2.0 copy-start.1
  110.3 36.4 %copy-start.3 = (bf16[256,768]{1,0:T(8,128)(2,1)S(1)}, bf16[256,768]{1,0:T(8,128)(2,1)}, u32[]{:S(2)}) copy-start(bf16[256,768]{1,0:T(8,128)(2,1)} %param.14) | copy-start | bytes 1179652
  110.3 60.5 %all-gather.5.cloned.1.call-start = ((), (), s32[]{:S(2)}) async-start(), calls=%async_computation.4 | async-start | bytes 1966080 | tf_op jit(solution)/shard_map/all_gather | solution.py:68
  148.3 22.5 %copy-start.2 = (bf16[256,768]{1,0:T(8,128)(2,1)}, bf16[256,768]{1,0:T(8,128)(2,1)S(1)}, u32[]{:S(2)}) copy-start(bf16[256,768]{1,0:T(8,128)(2,1)S(1)} %fusion.44) | copy-start | bytes 1179652
  151.0 140.3 %reduce-scatter.5.cloned.1.call-start = ((), (), s32[]{:S(2)}) async-start(), calls=%async_computation.5 | async-start | bytes 3538944 | tf_op jit(solution)/shard_map/reduce_scatter | solution.py:86
Sparse Core Ops, SparseCore 0:
  10.2 46.8 all-gather.2
  110.4 36.2 reduce-scatter.2
  151.1 19.6 all-gather.4
  216.7 74.5 reduce-scatter.4
where the time goes:
time: 300 us; the launch traced here: 299 us
  waiting for transfers between devices  175 us (58%)
  matrix products  75.7 us (25%)
  local copies, waits for them, and re-layouts  26.1 us (9%)
  between operations  14.5 us (5%)
  other arithmetic  7.68 us (3%)
    reduce_scatter x1, waiting for transfers between devices, per_device(): lax.psum_scatter(author_part.reshape(col_blocks * side, width), 'prow', s...  74.7 us
    all_gather x1, waiting for transfers between devices, per_device(): authors = lax.all_gather(author_x, 'prow', axis=0, tiled=True)  43.8 us
    reduce_scatter x1, waiting for transfers between devices, per_device(): lax.psum_scatter(partial_value, 'pcol', scatter_dimension=0, tiled=True)  36.3 us
    dot_general x2, matrix products, second_hop(): jnp.einsum('kc,kaf->caf', placing, product, precision=lax.Precision.HIGHEST)  22.4 us
    dot_general x2, matrix products, first_hop(): jnp.einsum('kr,kpf->rpf', placing, product, precision=lax.Precision.HIGHEST)  22.3 us
    all_gather x1, waiting for transfers between devices, per_device(): lax.all_gather(outgoing, 'pcol', axis=0, tiled=True)  19.5 us
    dot_general x2, matrix products, second_hop(): jnp.einsum('kpa,kpf->kaf', content_now, picked, preferred_element_type=jn...  11.1 us
    dot_general x2, matrix products, first_hop(): jnp.einsum('kpa,kaf->kpf', content_now, picked, preferred_element_type=jn...  11 us
  transfers between devices with their start and end apart: 4, of which 4 were waited for; matrix products, arithmetic and copies ran while one was open for 2% of the time, Pallas kernels for 0%

commit v1 on v0

v1 whole, which is shorter than its diff:
```python
import functools

import jax
import jax.numpy as jnp
from jax import lax
from jax.experimental import pallas as pl
from jax.experimental.pallas import tpu as pltpu
from jax.sharding import PartitionSpec as P

MESH = pl.DeviceIdType.MESH
F32 = jnp.float32
BF16 = jnp.bfloat16


def dot(a, b):
    return jnp.dot(a, b, preferred_element_type=F32)


def kernel(
    n_prow, n_pcol, tile,
    tab, author, paper_h, w_self_h, w_rel_h, w_two_h, blocks_h,
    hidden, author_out,
    paper, w_self, w_rel, w_two, blocks,
    x_all, msgs, dense, dense_t, self_term,
    pair_out, pair_in, x_out, x_in, acc,
    rows_all, y_out, y_in, y_acc, z_out, z_in,
    local_sem,
    g_send, g_recv, gy_send, gy_recv,
    pair_s, pair_r, xs, xr,
    o_send, o_recv, oc_send, oc_recv,
    ys, yr, zs, zr,
):
    i = lax.axis_index("prow")
    j = lax.axis_index("pcol")
    z, y = i // 2, i % 2
    x, c = j // 2, j % 2
    H, G = n_prow // 2, n_pcol // 2
    own_papers, width = paper.shape
    own_authors = author.shape[0]
    side = blocks.shape[1]
    authors = own_authors * n_prow
    papers = own_papers * n_pcol
    nf = width // tile
    y_part = z * 2 + 1 - y
    c_part = x * 2 + 1 - c

    waits = []

    def send(cond, src, dst, ss, rs, di, dj):
        def desc():
            return pltpu.make_async_remote_copy(
                src_ref=src, dst_ref=dst, send_sem=ss, recv_sem=rs,
                device_id=(di, dj), device_id_type=MESH,
            )

        if cond is None:
            desc().start()
        else:
            @pl.when(cond)
            def _():
                desc().start()
        waits.append((cond, desc))

    def arrive(dst, ss, rs):
        pltpu.make_async_remote_copy(
            src_ref=dst, dst_ref=dst, send_sem=ss, recv_sem=rs,
            device_id=(i, c_part), device_id_type=MESH,
        ).wait_recv()

    loads = [
        pltpu.make_async_copy(src, dst, local_sem.at[n])
        for n, (src, dst) in enumerate(
            ((blocks_h, blocks), (w_rel_h, w_rel), (paper_h, paper), (w_self_h, w_self), (w_two_h, w_two))
        )
    ]
    for load in loads:
        load.start()

    barrier = pltpu.get_barrier_semaphore()

    def greet(cond, di, dj):
        def go():
            pl.semaphore_signal(barrier, inc=1, device_id=(di, dj), device_id_type=MESH)

        if cond is None:
            go()
        else:
            pl.when(cond)(go)

    up_z, down_z, up_x, down_x = z < H - 1, z > 0, x < G - 1, x > 0
    greet(None, y_part, j)
    greet(None, i, c_part)
    greet(up_z, i + 2, j)
    greet(down_z, i - 2, j)
    greet(up_x, i, j + 2)
    greet(down_x, i, j - 2)
    peers = 2
    for cond in (up_z, down_z, up_x, down_x):
        peers = peers + cond.astype(jnp.int32)
    pl.semaphore_wait(barrier, peers)

    send(up_z, author, x_all.at[z, y], g_send.at[0, 0], g_recv.at[0, 0], i + 2, j)
    send(down_z, author, x_all.at[z, y], g_send.at[1, 0], g_recv.at[1, 0], i - 2, j)
    send(None, author, x_all.at[z, y], gy_send.at[2, 0], gy_recv.at[2, 0], y_part, j)
    x_all[z, y] = author[...]

    loads[0].wait()
    row_blocks, col_blocks = papers // side, authors // side
    p_step, a_step = min(side, own_papers), min(side, own_authors)
    for rb in range(row_blocks):
        for cb in range(col_blocks):
            pos = rb * col_blocks + cb
            slot, kind = tab[0, pos], tab[1, pos]
            block = blocks[slot].astype(F32)
            for t in range(2):
                part = (block * (kind == t).astype(F32)).astype(BF16)
                lo = t * authors + cb * side
                for sub in range(side // p_step):
                    row = rb * side + sub * p_step
                    dense[row // own_papers, row % own_papers:row % own_papers + p_step, lo:lo + side] = part[
                        sub * p_step:(sub + 1) * p_step
                    ]
            flip = (block * (kind < 2).astype(F32)).T.astype(BF16)
            for sub in range(side // a_step):
                owner = (cb * side + sub * a_step) // own_authors
                dense_t[owner % 2, owner // 2, :, rb * side:(rb + 1) * side] = flip[sub * a_step:(sub + 1) * a_step]

    loads[2].wait()
    loads[3].wait()
    for f in range(nf):
        cols = slice(f * tile, (f + 1) * tile)
        self_term[:, cols] = dot(paper[...], w_self[:, cols])
    loads[1].wait()
    loads[4].wait()

    def message_pair(zz):
        pair = x_all[zz].reshape(2 * own_authors, width)
        for t in range(2):
            @pl.loop(0, nf)
            def _(n):
                cols = pl.ds(pl.multiple_of(n * tile, tile), tile)
                msgs[t, zz, :, cols] = dot(pair, w_rel[t, :, cols]).astype(BF16)

    def z_arrival(s):
        below, above = z - 1 - s, z + 1 + s

        @pl.when(below >= 0)
        def _():
            arrive(x_all.at[below, y], g_send.at[0, s], g_recv.at[0, s])

        if s + 1 <= H - 2:
            send((below >= 0) & up_z, x_all.at[below, y], x_all.at[below, y],
                 g_send.at[0, s + 1], g_recv.at[0, s + 1], i + 2, j)
        send(below >= 0, x_all.at[below, y], x_all.at[below, y], gy_send.at[0, s], gy_recv.at[0, s], y_part, j)

        @pl.when(above <= H - 1)
        def _():
            arrive(x_all.at[above, y], g_send.at[1, s], g_recv.at[1, s])

        if s + 1 <= H - 2:
            send((above <= H - 1) & down_z, x_all.at[above, y], x_all.at[above, y],
                 g_send.at[1, s + 1], g_recv.at[1, s + 1], i - 2, j)
        send(above <= H - 1, x_all.at[above, y], x_all.at[above, y], gy_send.at[1, s], gy_recv.at[1, s], y_part, j)

    def y_arrival(s):
        below, above = z - 1 - s, z + 1 + s

        @pl.when(below >= 0)
        def _():
            arrive(x_all.at[below, 1 - y], gy_send.at[0, s], gy_recv.at[0, s])
            message_pair(below)

        @pl.when(above <= H - 1)
        def _():
            arrive(x_all.at[above, 1 - y], gy_send.at[1, s], gy_recv.at[1, s])
            message_pair(above)

    for s in range(H - 1):
        z_arrival(s)
        if s == 0:
            arrive(x_all.at[z, 1 - y], gy_send.at[2, 0], gy_recv.at[2, 0])
            message_pair(z)
        else:
            y_arrival(s - 1)
    y_arrival(H - 2)

    def first_hop(q, f):
        cols = slice(f * tile, (f + 1) * tile)
        return dot(dense[q], msgs[:, :, :, cols].reshape(2 * authors, tile))

    for d in range(1, G + 1):
        b = lax.rem(x + d, G)
        for f in range(nf):
            pair_out[d - 1, f] = first_hop(b * 2 + 1 - c, f).astype(BF16)
            send(None, pair_out.at[d - 1, f], pair_in.at[d - 1, f], pair_s.at[d - 1, f], pair_r.at[d - 1, f], i, c_part)
        for f in range(nf):
            acc[f] = first_hop(b * 2 + c, f)
            arrive(pair_in.at[d - 1, f], pair_s.at[d - 1, f], pair_r.at[d - 1, f])
            acc[f] = acc[f] + pair_in[d - 1, f].astype(F32)
            if d == G:
                continue
            is_up, is_down = b > x, b < x

            @pl.when(is_up & (x > 0))
            def _():
                arrive(x_in.at[0, b, f], xs.at[0, b, f], xr.at[0, b, f])
                acc[f] = acc[f] + x_in[0, b, f].astype(F32)

            @pl.when(is_down & (x < G - 1))
            def _():
                arrive(x_in.at[1, b, f], xs.at[1, b, f], xr.at[1, b, f])
                acc[f] = acc[f] + x_in[1, b, f].astype(F32)

            x_out[d - 1, f] = acc[f].astype(BF16)
            send(is_up, x_out.at[d - 1, f], x_in.at[0, b, f], xs.at[0, b, f], xr.at[0, b, f], i, j + 2)
            send(is_down, x_out.at[d - 1, f], x_in.at[1, b, f], xs.at[1, b, f], xr.at[1, b, f], i, j - 2)

    for f in range(nf):
        cols = slice(f * tile, (f + 1) * tile)

        @pl.when(x > 0)
        def _():
            arrive(x_in.at[0, x, f], xs.at[0, x, f], xr.at[0, x, f])
            acc[f] = acc[f] + x_in[0, x, f].astype(F32)

        @pl.when(x < G - 1)
        def _():
            arrive(x_in.at[1, x, f], xs.at[1, x, f], xr.at[1, x, f])
            acc[f] = acc[f] + x_in[1, x, f].astype(F32)

        hidden[:, cols] = jnp.maximum(acc[f] + self_term[:, cols], 0.0).astype(BF16)

    for f in range(nf):
        cols = slice(f * tile, (f + 1) * tile)
        rows_all[f, x, c] = dot(hidden[...], w_two[:, cols]).astype(BF16)
        own = rows_all.at[f, x, c]
        send(up_x, own, own, o_send.at[0, 0, f], o_recv.at[0, 0, f], i, j + 2)
        send(down_x, own, own, o_send.at[1, 0, f], o_recv.at[1, 0, f], i, j - 2)
        send(None, own, own, oc_send.at[2, 0, f], oc_recv.at[2, 0, f], i, c_part)

    def pass_on(f):
        for s in range(G - 1):
            below, above = x - 1 - s, x + 1 + s

            @pl.when(below >= 0)
            def _():
                arrive(rows_all.at[f, below, c], o_send.at[0, s, f], o_recv.at[0, s, f])

            part = rows_all.at[f, below, c]
            if s + 1 <= G - 2:
                send((below >= 0) & up_x, part, part, o_send.at[0, s + 1, f], o_recv.at[0, s + 1, f], i, j + 2)
            send(below >= 0, part, part, oc_send.at[0, s, f], oc_recv.at[0, s, f], i, c_part)

            @pl.when(above <= G - 1)
            def _():
                arrive(rows_all.at[f, above, c], o_send.at[1, s, f], o_recv.at[1, s, f])

            part = rows_all.at[f, above, c]
            if s + 1 <= G - 2:
                send((above <= G - 1) & down_x, part, part, o_send.at[1, s + 1, f], o_recv.at[1, s + 1, f], i, j - 2)
            send(above <= G - 1, part, part, oc_send.at[1, s, f], oc_recv.at[1, s, f], i, c_part)

    def collect(f):
        arrive(rows_all.at[f, x, 1 - c], oc_send.at[2, 0, f], oc_recv.at[2, 0, f])
        for s in range(G - 1):
            below, above = x - 1 - s, x + 1 + s

            @pl.when(below >= 0)
            def _():
                arrive(rows_all.at[f, below, 1 - c], oc_send.at[0, s, f], oc_recv.at[0, s, f])

            @pl.when(above <= G - 1)
            def _():
                arrive(rows_all.at[f, above, 1 - c], oc_send.at[1, s, f], oc_recv.at[1, s, f])

    for f in range(nf):
        pass_on(f)
        collect(f)
        table = rows_all[f].reshape(papers, tile)
        far = dot(dense_t[1 - y].reshape(H * own_authors, papers), table)
        y_out[f] = far.astype(BF16).reshape(H, own_authors, tile)
        send(None, y_out.at[f], y_in.at[f], ys.at[f], yr.at[f], y_part, j)
        near = dot(dense_t[y].reshape(H * own_authors, papers), table)
        y_acc[f] = near.reshape(H, own_authors, tile)

    for f in range(nf):
        arrive(y_in.at[f], ys.at[f], yr.at[f])
        y_acc[f] = y_acc[f] + y_in[f].astype(F32)
        for s in range(H - 1):
            for way, b in ((0, H - 1 - s), (1, s)):
                cond = (z < b) if way == 0 else (z > b)
                first = (z == 0) if way == 0 else (z == H - 1)

                @pl.when(cond & first)
                def _():
                    z_out[way, f, b] = y_acc[f, b].astype(BF16)

                @pl.when(cond & jnp.logical_not(first))
                def _():
                    arrive(z_in.at[way, f, b], zs.at[way, f, b], zr.at[way, f, b])
                    z_out[way, f, b] = (y_acc[f, b] + z_in[way, f, b].astype(F32)).astype(BF16)

                send(cond, z_out.at[way, f, b], z_in.at[way, f, b], zs.at[way, f, b], zr.at[way, f, b],
                     i + 2 if way == 0 else i - 2, j)

    for f in range(nf):
        cols = slice(f * tile, (f + 1) * tile)
        total = y_acc.at[f, z]

        @pl.when(z > 0)
        def _():
            arrive(z_in.at[0, f, z], zs.at[0, f, z], zr.at[0, f, z])
            total[...] = total[...] + z_in[0, f, z].astype(F32)

        @pl.when(z < H - 1)
        def _():
            arrive(z_in.at[1, f, z], zs.at[1, f, z], zr.at[1, f, z])
            total[...] = total[...] + z_in[1, f, z].astype(F32)

        author_out[:, cols] = total[...].astype(BF16)

    for cond, desc in waits:
        if cond is None:
            desc().wait_send()
        else:
            @pl.when(cond)
            def _():
                desc().wait_send()


def per_device(
    n_prow, n_pcol, paper_x, author_x, w_self, w_rel, w_two,
    block_rows, block_cols, block_type, block_count, block_vals,
):
    slots, side = block_vals.shape[2], block_vals.shape[3]
    own_papers, width = paper_x.shape
    own_authors = author_x.shape[0]
    papers, authors = own_papers * n_pcol, own_authors * n_prow
    col_blocks = authors // side
    places = (papers // side) * col_blocks
    H, G = n_prow // 2, n_pcol // 2
    tile = 256 if width % 256 == 0 else 128
    nf = width // tile

    slot = jnp.arange(slots, dtype=jnp.int32)
    where = block_rows.reshape(slots) * col_blocks + block_cols.reshape(slots)
    live = slot < block_count.reshape(())
    hit = (where[:, None] == jnp.arange(places, dtype=jnp.int32)[None, :]) & live[:, None]
    which = jnp.sum(jnp.where(hit, slot[:, None], 0), axis=0)
    kind = 2 + jnp.sum(jnp.where(hit, block_type.reshape(slots)[:, None] - 2, 0), axis=0)
    tab = jnp.stack([which, kind]).astype(jnp.int32)

    vmem, anyspace, smem = pltpu.VMEM, pl.ANY, pltpu.SMEM
    dma = pltpu.SemaphoreType.DMA
    hz, gx = max(H - 1, 1), max(G - 1, 1)
    return pl.pallas_call(
        functools.partial(kernel, n_prow, n_pcol, tile),
        out_shape=(
            jax.ShapeDtypeStruct((own_papers, width), BF16),
            jax.ShapeDtypeStruct((own_authors, width), BF16),
        ),
        in_specs=[pl.BlockSpec(memory_space=smem), pl.BlockSpec(memory_space=vmem)]
        + [pl.BlockSpec(memory_space=anyspace)] * 5,
        out_specs=(pl.BlockSpec(memory_space=vmem),) * 2,
        scratch_shapes=[
            vmem((own_papers, width), BF16),
            vmem((width, width), BF16),
            vmem(w_rel.shape, BF16),
            vmem((width, width), BF16),
            vmem((slots, side, side), BF16),
            vmem((H, 2, own_authors, width), BF16),
            vmem((2, H, 2 * own_authors, width), BF16),
            vmem((n_pcol, own_papers, 2 * authors), BF16),
            vmem((2, H, own_authors, papers), BF16),
            vmem((own_papers, width), F32),
            vmem((G, nf, own_papers, tile), BF16),
            vmem((G, nf, own_papers, tile), BF16),
            vmem((gx, nf, own_papers, tile), BF16),
            vmem((2, G, nf, own_papers, tile), BF16),
            vmem((nf, own_papers, tile), F32),
            vmem((nf, G, 2, own_papers, tile), BF16),
            vmem((nf, H, own_authors, tile), BF16),
            vmem((nf, H, own_authors, tile), BF16),
            vmem((nf, H, own_authors, tile), F32),
            vmem((2, nf, H, own_authors, tile), BF16),
            vmem((2, nf, H, own_authors, tile), BF16),
            dma((5,)),
            dma((2, hz)), dma((2, hz)), dma((3, hz)), dma((3, hz)),
            dma((G, nf)), dma((G, nf)), dma((2, G, nf)), dma((2, G, nf)),
            dma((2, gx, nf)), dma((2, gx, nf)), dma((3, gx, nf)), dma((3, gx, nf)),
            dma((nf,)), dma((nf,)), dma((2, nf, H)), dma((2, nf, H)),
        ],
        compiler_params=pltpu.CompilerParams(
            collective_id=0, has_side_effects=True, vmem_limit_bytes=60 * 1024 * 1024
        ),
    )(tab, author_x, paper_x, w_self, w_rel, w_two, block_vals.reshape(slots, side, side))


def solution(mesh):
    return jax.shard_map(
        functools.partial(per_device, mesh.shape["prow"], mesh.shape["pcol"]),
        mesh=mesh,
        in_specs=(
            P(("prow", "pcol"), None),
            P(("pcol", "prow"), None),
            P(),
            P(),
            P(),
            P("prow", "pcol", None),
            P("prow", "pcol", None),
            P("prow", "pcol", None),
            P("prow", "pcol"),
            P("prow", "pcol", None, None, None),
        ),
        out_specs=(P(("prow", "pcol"), None), P(("pcol", "prow"), None)),
        check_vma=False,
    )
```

time: 300 us -> 92.4 us (0.31)
  waiting for transfers between devices: 175 us -> 0 us
  Pallas kernels: 0 us -> 86.1 us
  matrix products: 75.7 us -> 0 us
  local copies, waits for them, and re-layouts: 26.1 us -> 3.38 us
  between operations: 14.5 us -> 1.3 us
  other arithmetic: 7.68 us -> 1.37 us
    reduce_scatter x2 -> x0, waiting for transfers between devices: 111 us -> none  [the longest x1 74.7 us: per_device(): lax.psum_scatter(author_part.reshape(col_blocks * side, width), 'prow', s...]
    pallas_call x0 -> x1, Pallas kernels: none -> 86.1 us  [per_device(): pl.pallas_call(functools.partial(kernel, n_prow, n_pcol, tile), out_shape...]
    dot_general x12 -> x0, matrix products: 75.7 us -> none  [the longest x2 22.4 us: second_hop(): jnp.einsum('kc,kaf->caf', placing, product, precision=lax.Precision.HIGHEST)]
    all_gather x2 -> x0, waiting for transfers between devices: 63.3 us -> none  [the longest x1 43.8 us: per_device(): authors = lax.all_gather(author_x, 'prow', axis=0, tiled=True)]
    gather x4 -> x0, local copies, waits for them, and re-layouts: 16.1 us -> none  [the longest x2 8.54 us: first_hop(): picked = table[types_now * col_blocks + cols_now]]
    while x2 -> x0, local copies, waits for them, and re-layouts: 9.11 us -> none  [the longest x1 4.56 us: per_device(): lax.scan(second_hop, start_two, (row_ids, col_ids, live, contents))]
    unnamed x5 -> x0, other arithmetic: 3.96 us -> none
  transfers between devices with their start and end apart: 4 -> 0, of which waited for: 4 -> 0; matrix products, arithmetic and copies ran while one was open for 2% -> 0% of each run, Pallas kernels for 0% -> 0%
where the time goes in v1:
time: 92.4 us; the launch traced here: 92.2 us
  Pallas kernels  86.1 us (93%)
  local copies, waits for them, and re-layouts  3.38 us (4%)
  other arithmetic  1.37 us (1%)
  between operations  1.3 us (1%)
    pallas_call x1, Pallas kernels, per_device(): pl.pallas_call(functools.partial(kernel, n_prow, n_pcol, tile), out_shape...  86.1 us
    unnamed x2, local copies, waits for them, and re-layouts  3.38 us

profile of v1, /device:TPU:0, one launch (start us, length us, event | category | flops | bytes accessed | tf_op | source)
XLA Modules:
  0.0 92.2 jit_solution(15670258864099839902)
XLA Ops:
  1.3 0.7 add_bitcast_fusion.1
  2.0 0.1 select_reduce_fusion.1
  2.1 0.6 pad_add_fusion.tab
  2.7 86.1 %shard_map.113 = (bf16[256,768]{1,0:T(8,128)(2,1)}, bf16[128,768]{1,0:T(8,128)(2,1)}) custom-call(s32[2,64]{1,0:T(2,128)} %pad_add_fusion.tab, bf16[128,768]{1,0:T(8,128)(2,1)} %author.1, bf16[256,768]{1,0:T(8,128)(2,1)} %paper_h.1, bf16[768,768]{1,0:T(8,128)(2,1)} %w_self_h.1, bf16[2,768,768]{2,1,0:T(8,128)(2,1)} %w_rel_h.1, bf16[768,768]{1,0:T(8,128)(2,1)} %w_two_h.1, ...), custom_call_target="tpu_custom_call" | custom-call | tf_op jit(solution)/shard_map/pallas_call | solution.py:356
  88.8 1.8 %copy.15 = bf16[256,768]{1,0:T(8,128)(2,1)} copy(bf16[256,768]{1,0:T(8,128)(2,1)} %get-tuple-element.8) | data formatting | bytes 786432
  90.5 1.6 %copy.16 = bf16[128,768]{1,0:T(8,128)(2,1)} copy(bf16[128,768]{1,0:T(8,128)(2,1)} %get-tuple-element.9) | data formatting | bytes 393216
  (2 shorter events, 0.0 us)

commit v2 on v1

--- a/solution.py
+++ b/solution.py
@@ -99,39 +99,41 @@
         peers = peers + cond.astype(jnp.int32)
     pl.semaphore_wait(barrier, peers)
 
-    send(up_z, author, x_all.at[z, y], g_send.at[0, 0], g_recv.at[0, 0], i + 2, j)
-    send(down_z, author, x_all.at[z, y], g_send.at[1, 0], g_recv.at[1, 0], i - 2, j)
-    send(None, author, x_all.at[z, y], gy_send.at[2, 0], gy_recv.at[2, 0], y_part, j)
+    parts = g_send.shape[2]
+    part_rows = own_authors // parts
+
+    def piece(zz, yy, h):
+        return x_all.at[zz, yy, pl.ds(h * part_rows, part_rows), :]
+
+    for h in range(parts):
+        mine = author.at[pl.ds(h * part_rows, part_rows), :]
+        send(up_z, mine, piece(z, y, h), g_send.at[0, 0, h], g_recv.at[0, 0, h], i + 2, j)
+        send(down_z, mine, piece(z, y, h), g_send.at[1, 0, h], g_recv.at[1, 0, h], i - 2, j)
+        send(None, mine, piece(z, y, h), gy_send.at[2, 0, h], gy_recv.at[2, 0, h], y_part, j)
     x_all[z, y] = author[...]
 
     loads[0].wait()
     row_blocks, col_blocks = papers // side, authors // side
     p_step, a_step = min(side, own_papers), min(side, own_authors)
-    for rb in range(row_blocks):
-        for cb in range(col_blocks):
-            pos = rb * col_blocks + cb
-            slot, kind = tab[0, pos], tab[1, pos]
-            block = blocks[slot].astype(F32)
-            for t in range(2):
-                part = (block * (kind == t).astype(F32)).astype(BF16)
-                lo = t * authors + cb * side
-                for sub in range(side // p_step):
-                    row = rb * side + sub * p_step
-                    dense[row // own_papers, row % own_papers:row % own_papers + p_step, lo:lo + side] = part[
-                        sub * p_step:(sub + 1) * p_step
-                    ]
-            flip = (block * (kind < 2).astype(F32)).T.astype(BF16)
-            for sub in range(side // a_step):
-                owner = (cb * side + sub * a_step) // own_authors
-                dense_t[owner % 2, owner // 2, :, rb * side:(rb + 1) * side] = flip[sub * a_step:(sub + 1) * a_step]
-
-    loads[2].wait()
-    loads[3].wait()
-    for f in range(nf):
-        cols = slice(f * tile, (f + 1) * tile)
-        self_term[:, cols] = dot(paper[...], w_self[:, cols])
-    loads[1].wait()
-    loads[4].wait()
+
+    def densify(first, last):
+        for rb in range(first, last):
+            for cb in range(col_blocks):
+                pos = rb * col_blocks + cb
+                slot, kind = tab[0, pos], tab[1, pos]
+                block = blocks[slot].astype(F32)
+                for t in range(2):
+                    part = (block * (kind == t).astype(F32)).astype(BF16)
+                    lo = t * authors + cb * side
+                    for sub in range(side // p_step):
+                        row = rb * side + sub * p_step
+                        dense[row // own_papers, row % own_papers:row % own_papers + p_step, lo:lo + side] = part[
+                            sub * p_step:(sub + 1) * p_step
+                        ]
+                flip = (block * (kind < 2).astype(F32)).T.astype(BF16)
+                for sub in range(side // a_step):
+                    owner = (cb * side + sub * a_step) // own_authors
+                    dense_t[owner % 2, owner // 2, :, rb * side:(rb + 1) * side] = flip[sub * a_step:(sub + 1) * a_step]
 
     def message_pair(zz):
         pair = x_all[zz].reshape(2 * own_authors, width)
@@ -142,47 +144,49 @@
                 msgs[t, zz, :, cols] = dot(pair, w_rel[t, :, cols]).astype(BF16)
 
     def z_arrival(s):
-        below, above = z - 1 - s, z + 1 + s
-
-        @pl.when(below >= 0)
-        def _():
-            arrive(x_all.at[below, y], g_send.at[0, s], g_recv.at[0, s])
-
-        if s + 1 <= H - 2:
-            send((below >= 0) & up_z, x_all.at[below, y], x_all.at[below, y],
-                 g_send.at[0, s + 1], g_recv.at[0, s + 1], i + 2, j)
-        send(below >= 0, x_all.at[below, y], x_all.at[below, y], gy_send.at[0, s], gy_recv.at[0, s], y_part, j)
-
-        @pl.when(above <= H - 1)
-        def _():
-            arrive(x_all.at[above, y], g_send.at[1, s], g_recv.at[1, s])
-
-        if s + 1 <= H - 2:
-            send((above <= H - 1) & down_z, x_all.at[above, y], x_all.at[above, y],
-                 g_send.at[1, s + 1], g_recv.at[1, s + 1], i - 2, j)
-        send(above <= H - 1, x_all.at[above, y], x_all.at[above, y], gy_send.at[1, s], gy_recv.at[1, s], y_part, j)
+        for h in range(parts):
+            for way, near, inside, more, to in (
+                (0, z - 1 - s, z - 1 - s >= 0, up_z, i + 2),
+                (1, z + 1 + s, z + 1 + s <= H - 1, down_z, i - 2),
+            ):
+                part = piece(near, y, h)
+
+                @pl.when(inside)
+                def _():
+                    arrive(part, g_send.at[way, s, h], g_recv.at[way, s, h])
+
+                if s + 1 <= H - 2:
+                    send(inside & more, part, part, g_send.at[way, s + 1, h], g_recv.at[way, s + 1, h], to, j)
+                send(inside, part, part, gy_send.at[way, s, h], gy_recv.at[way, s, h], y_part, j)
 
     def y_arrival(s):
-        below, above = z - 1 - s, z + 1 + s
-
-        @pl.when(below >= 0)
-        def _():
-            arrive(x_all.at[below, 1 - y], gy_send.at[0, s], gy_recv.at[0, s])
-            message_pair(below)
-
-        @pl.when(above <= H - 1)
-        def _():
-            arrive(x_all.at[above, 1 - y], gy_send.at[1, s], gy_recv.at[1, s])
-            message_pair(above)
-
-    for s in range(H - 1):
+        for way, near, inside in ((0, z - 1 - s, z - 1 - s >= 0), (1, z + 1 + s, z + 1 + s <= H - 1)):
+            @pl.when(inside)
+            def _():
+                for h in range(parts):
+                    arrive(piece(near, 1 - y, h), gy_send.at[way, s, h], gy_recv.at[way, s, h])
+                message_pair(near)
+
+    densify(0, row_blocks // 2)
+    z_arrival(0)
+    densify(row_blocks // 2, row_blocks)
+    if H > 2:
+        z_arrival(1)
+    loads[2].wait()
+    loads[3].wait()
+    for f in range(nf):
+        cols = slice(f * tile, (f + 1) * tile)
+        self_term[:, cols] = dot(paper[...], w_self[:, cols])
+    loads[1].wait()
+    loads[4].wait()
+    for h in range(parts):
+        arrive(piece(z, 1 - y, h), gy_send.at[2, 0, h], gy_recv.at[2, 0, h])
+    message_pair(z)
+    for s in range(2, H - 1):
         z_arrival(s)
-        if s == 0:
-            arrive(x_all.at[z, 1 - y], gy_send.at[2, 0], gy_recv.at[2, 0])
-            message_pair(z)
-        else:
-            y_arrival(s - 1)
-    y_arrival(H - 2)
+        y_arrival(s - 2)
+    for s in range(max(H - 3, 0), H - 1):
+        y_arrival(s)
 
     def first_hop(q, f):
         cols = slice(f * tile, (f + 1) * tile)
@@ -279,26 +283,33 @@
         table = rows_all[f].reshape(papers, tile)
         far = dot(dense_t[1 - y].reshape(H * own_authors, papers), table)
         y_out[f] = far.astype(BF16).reshape(H, own_authors, tile)
-        send(None, y_out.at[f], y_in.at[f], ys.at[f], yr.at[f], y_part, j)
+        for s in range(H - 1):
+            for b, cond in ((H - 1 - s, z < H - 1 - s), (s, z > s)):
+                send(cond, y_out.at[f, b], y_in.at[f, b], ys.at[f, b], yr.at[f, b], y_part, j)
         near = dot(dense_t[y].reshape(H * own_authors, papers), table)
         y_acc[f] = near.reshape(H, own_authors, tile)
-
-    for f in range(nf):
-        arrive(y_in.at[f], ys.at[f], yr.at[f])
-        y_acc[f] = y_acc[f] + y_in[f].astype(F32)
+    for f in range(nf):
+        send(None, y_out.at[f, z], y_in.at[f, z], ys.at[f, z], yr.at[f, z], y_part, j)
+
+    for f in range(nf):
         for s in range(H - 1):
             for way, b in ((0, H - 1 - s), (1, s)):
                 cond = (z < b) if way == 0 else (z > b)
                 first = (z == 0) if way == 0 else (z == H - 1)
 
-                @pl.when(cond & first)
+                @pl.when(cond)
                 def _():
-                    z_out[way, f, b] = y_acc[f, b].astype(BF16)
+                    arrive(y_in.at[f, b], ys.at[f, b], yr.at[f, b])
+                    y_acc[f, b] = y_acc[f, b] + y_in[f, b].astype(F32)
 
                 @pl.when(cond & jnp.logical_not(first))
                 def _():
                     arrive(z_in.at[way, f, b], zs.at[way, f, b], zr.at[way, f, b])
-                    z_out[way, f, b] = (y_acc[f, b] + z_in[way, f, b].astype(F32)).astype(BF16)
+                    y_acc[f, b] = y_acc[f, b] + z_in[way, f, b].astype(F32)
+
+                @pl.when(cond)
+                def _():
+                    z_out[way, f, b] = y_acc[f, b].astype(BF16)
 
                 send(cond, z_out.at[way, f, b], z_in.at[way, f, b], zs.at[way, f, b], zr.at[way, f, b],
                      i + 2 if way == 0 else i - 2, j)
@@ -306,6 +317,8 @@
     for f in range(nf):
         cols = slice(f * tile, (f + 1) * tile)
         total = y_acc.at[f, z]
+        arrive(y_in.at[f, z], ys.at[f, z], yr.at[f, z])
+        total[...] = total[...] + y_in[f, z].astype(F32)
 
         @pl.when(z > 0)
         def _():
@@ -385,10 +398,10 @@
             vmem((2, nf, H, own_authors, tile), BF16),
             vmem((2, nf, H, own_authors, tile), BF16),
             dma((5,)),
-            dma((2, hz)), dma((2, hz)), dma((3, hz)), dma((3, hz)),
+            dma((2, hz, 2)), dma((2, hz, 2)), dma((3, hz, 2)), dma((3, hz, 2)),
             dma((G, nf)), dma((G, nf)), dma((2, G, nf)), dma((2, G, nf)),
             dma((2, gx, nf)), dma((2, gx, nf)), dma((3, gx, nf)), dma((3, gx, nf)),
-            dma((nf,)), dma((nf,)), dma((2, nf, H)), dma((2, nf, H)),
+            dma((nf, H)), dma((nf, H)), dma((2, nf, H)), dma((2, nf, H)),
         ],
         compiler_params=pltpu.CompilerParams(
             collective_id=0, has_side_effects=True, vmem_limit_bytes=60 * 1024 * 1024

time: 92.4 us -> 87.8 us (0.950)
  Pallas kernels: 86.1 us -> 81.6 us
    pallas_call x1, Pallas kernels: 86.1 us -> 81.6 us  [per_device(): pl.pallas_call(functools.partial(kernel, n_prow, n_pcol, tile), out_shape...]
where the time goes in v2:
time: 87.8 us; the launch traced here: 87.6 us
  Pallas kernels  81.6 us (93%)
  local copies, waits for them, and re-layouts  3.38 us (4%)
  other arithmetic  1.37 us (2%)
  between operations  1.3 us (1%)
    pallas_call x1, Pallas kernels, per_device(): pl.pallas_call(functools.partial(kernel, n_prow, n_pcol, tile), out_shape...  81.6 us
    unnamed x2, local copies, waits for them, and re-layouts  3.38 us

profile of v2, /device:TPU:0, one launch (start us, length us, event | category | flops | bytes accessed | tf_op | source)
XLA Modules:
  0.0 87.6 jit_solution(6244503375450130803)
XLA Ops:
  1.3 0.7 add_bitcast_fusion.1
  2.0 0.1 select_reduce_fusion.1
  2.1 0.6 pad_add_fusion.tab
  2.7 81.6 %shard_map.113 = (bf16[256,768]{1,0:T(8,128)(2,1)}, bf16[128,768]{1,0:T(8,128)(2,1)}) custom-call(s32[2,64]{1,0:T(2,128)} %pad_add_fusion.tab, bf16[128,768]{1,0:T(8,128)(2,1)} %author.1, bf16[256,768]{1,0:T(8,128)(2,1)} %paper_h.1, bf16[768,768]{1,0:T(8,128)(2,1)} %w_self_h.1, bf16[2,768,768]{2,1,0:T(8,128)(2,1)} %w_rel_h.1, bf16[768,768]{1,0:T(8,128)(2,1)} %w_two_h.1, ...), custom_call_target="tpu_custom_call" | custom-call | tf_op jit(solution)/shard_map/pallas_call | solution.py:369
  84.2 1.8 %copy.15 = bf16[256,768]{1,0:T(8,128)(2,1)} copy(bf16[256,768]{1,0:T(8,128)(2,1)} %get-tuple-element.8) | data formatting | bytes 786432
  86.0 1.6 %copy.16 = bf16[128,768]{1,0:T(8,128)(2,1)} copy(bf16[128,768]{1,0:T(8,128)(2,1)} %get-tuple-element.9) | data formatting | bytes 393216
  (2 shorter events, 0.0 us)

commit v3 on v2

--- a/solution.py
+++ b/solution.py
@@ -277,6 +277,7 @@
             def _():
                 arrive(rows_all.at[f, above, 1 - c], oc_send.at[1, s, f], oc_recv.at[1, s, f])
 
+    low = z < H // 2
     for f in range(nf):
         pass_on(f)
         collect(f)
@@ -284,7 +285,7 @@
         far = dot(dense_t[1 - y].reshape(H * own_authors, papers), table)
         y_out[f] = far.astype(BF16).reshape(H, own_authors, tile)
         for s in range(H - 1):
-            for b, cond in ((H - 1 - s, z < H - 1 - s), (s, z > s)):
+            for b, cond in ((H - 1 - s, (z < H - 1 - s) & low), (s, z > s), (H - 1 - s, (z < H - 1 - s) & (z >= H // 2))):
                 send(cond, y_out.at[f, b], y_in.at[f, b], ys.at[f, b], yr.at[f, b], y_part, j)
         near = dot(dense_t[y].reshape(H * own_authors, papers), table)
         y_acc[f] = near.reshape(H, own_authors, tile)
@@ -293,8 +294,9 @@
 
     for f in range(nf):
         for s in range(H - 1):
-            for way, b in ((0, H - 1 - s), (1, s)):
-                cond = (z < b) if way == 0 else (z > b)
+            for way, b, cond in (
+                (0, H - 1 - s, (z < H - 1 - s) & low), (1, s, z > s), (0, H - 1 - s, (z < H - 1 - s) & (z >= H // 2))
+            ):
                 first = (z == 0) if way == 0 else (z == H - 1)
 
                 @pl.when(cond)

time: 87.8 us -> 79.6 us (0.907)
  Pallas kernels: 81.6 us -> 73.3 us
    pallas_call x1, Pallas kernels: 81.6 us -> 73.3 us  [per_device(): pl.pallas_call(functools.partial(kernel, n_prow, n_pcol, tile), out_shape...]
where the time goes in v3:
time: 79.6 us; the launch traced here: 79.4 us
  Pallas kernels  73.3 us (92%)
  local copies, waits for them, and re-layouts  3.38 us (4%)
  other arithmetic  1.37 us (2%)
  between operations  1.3 us (2%)
    pallas_call x1, Pallas kernels, per_device(): pl.pallas_call(functools.partial(kernel, n_prow, n_pcol, tile), out_shape...  73.3 us
    unnamed x2, local copies, waits for them, and re-layouts  3.38 us

profile of v3, /device:TPU:0, one launch (start us, length us, event | category | flops | bytes accessed | tf_op | source)
XLA Modules:
  0.0 79.4 jit_solution(221966270112591688)
XLA Ops:
  1.3 0.7 add_bitcast_fusion.1
  2.0 0.1 select_reduce_fusion.1
  2.1 0.6 pad_add_fusion.tab
  2.7 73.3 %shard_map.113 = (bf16[256,768]{1,0:T(8,128)(2,1)}, bf16[128,768]{1,0:T(8,128)(2,1)}) custom-call(s32[2,64]{1,0:T(2,128)} %pad_add_fusion.tab, bf16[128,768]{1,0:T(8,128)(2,1)} %author.1, bf16[256,768]{1,0:T(8,128)(2,1)} %paper_h.1, bf16[768,768]{1,0:T(8,128)(2,1)} %w_self_h.1, bf16[2,768,768]{2,1,0:T(8,128)(2,1)} %w_rel_h.1, bf16[768,768]{1,0:T(8,128)(2,1)} %w_two_h.1, ...), custom_call_target="tpu_custom_call" | custom-call | tf_op jit(solution)/shard_map/pallas_call | solution.py:371
  76.0 1.8 %copy.15 = bf16[256,768]{1,0:T(8,128)(2,1)} copy(bf16[256,768]{1,0:T(8,128)(2,1)} %get-tuple-element.8) | data formatting | bytes 786432
  77.8 1.6 %copy.16 = bf16[128,768]{1,0:T(8,128)(2,1)} copy(bf16[128,768]{1,0:T(8,128)(2,1)} %get-tuple-element.9) | data formatting | bytes 393216
  (2 shorter events, 0.0 us)
